TPU v7x, 512 devices: a whole 4x8x8 slice. The times are simulated.
512 devices in a mesh: dp: 8 (over y), expert: 64 (over x, z, core).
Axes of the slice: x: 4, y: 8, z: 8, core: 2. Of those that a mesh axis runs over, the one named last changes fastest.
Arguments:
- tokens: bfloat16 [8192, 4096], P('expert', 'dp'), may hold values from -6 to 6
- cotangent: bfloat16 [8192, 4096], P('expert', 'dp'), may hold values from -6 to 6
- expert_ids: int32 [8192, 6], P('expert'), may hold values from 0 to 63, all different within a row; in each aligned block of 128 rows (0 to 127, 128 to 255, ...) at most 14 rows name the same one
- route_probs: bfloat16 [8192, 6], P('expert'), may hold values from 0.049804688 to 1
- w_gate: bfloat16 [64, 4096, 768], P('expert', 'dp'), may hold values from -0.09375 to 0.09375
- w_up: bfloat16 [64, 4096, 768], P('expert', 'dp'), may hold values from -0.09375 to 0.09375
- w_down: bfloat16 [64, 768, 4096], P('expert', None, 'dp'), may hold values from -0.09375 to 0.09375
Outputs:
- grad_tokens: bfloat16 [8192, 4096], P('expert', 'dp')
- grad_gate: bfloat16 [64, 4096, 768], P('expert', 'dp')
- grad_up: bfloat16 [64, 4096, 768], P('expert', 'dp')
- grad_down: bfloat16 [64, 768, 4096], P('expert', None, 'dp')
- d_probs: bfloat16 [8192, 6], P('expert')
Inputs may be any that keep to these rules, and one draw needn't show every extreme that they name: `expert_ids`: each row names 6 different experts and every expert is named by some row; in each aligned block of 128 rows no expert is named by more than 14 rows, a bound that some block reaches.
All inputs are finite; a program needn't handle non-finite values.
Results may differ from a plain program's by a relative error of at most 0.024.
Values may be sent and summed in bfloat16 or wider, within the bound.
A program may use at most 64 MiB of HBM per device.

v0:
```python
import jax
import jax.numpy as jnp
from jax import lax
from jax.sharding import PartitionSpec as P


def silu_parts(gate_sum):
    logistic = jax.nn.sigmoid(gate_sum)
    return (gate_sum * logistic, logistic * (1.0 + gate_sum * (1.0 - logistic)))


def local_step(gate_sum, up_sum, grad_h, gate_probs):
    activated, derivative = silu_parts(gate_sum)
    hidden_f = lax.optimization_barrier((activated * up_sum).astype(jnp.bfloat16)).astype(
        jnp.float32
    )
    prob_grad = jnp.sum(hidden_f * grad_h, axis=1).astype(jnp.bfloat16)
    scaled = gate_probs[:, None] * grad_h
    d_gate = (scaled * up_sum * derivative).astype(jnp.bfloat16)
    d_up = (scaled * activated).astype(jnp.bfloat16)
    h_scaled = (gate_probs[:, None] * hidden_f).astype(jnp.bfloat16)
    return (h_scaled, d_gate, d_up, prob_grad)


def local(tokens, cotangent, expert_ids, route_probs, w_gate, w_up, w_down):
    expert_count = lax.axis_size("expert")
    token_count = tokens.shape[0]
    columns = tokens.shape[1]
    fanout = expert_ids.shape[1]
    capacity = max(2, 7 * token_count * fanout // (6 * expert_count))
    assigned = token_count * fanout
    rows_all = expert_count * capacity
    flat_ids = expert_ids.reshape(assigned)
    onehot = (flat_ids[:, None] == jnp.arange(expert_count, dtype=jnp.int32)[None, :]).astype(
        jnp.int32
    )
    earlier = jnp.cumsum(onehot, axis=0) - onehot
    slot_index = jnp.sum(earlier * onehot, axis=1)
    target = flat_ids * capacity + slot_index
    anchor = (
        jnp.full((rows_all,), assigned, jnp.int32)
        .at[target]
        .set(jnp.arange(assigned, dtype=jnp.int32))
    )
    token_of = anchor // fanout
    zero_row = jnp.zeros((1, columns), jnp.bfloat16)
    sent_x = jnp.concatenate([tokens, zero_row], axis=0)[token_of].reshape(
        expert_count, capacity, columns
    )
    sent_dy = jnp.concatenate([cotangent, zero_row], axis=0)[token_of].reshape(
        expert_count, capacity, columns
    )
    sent_p = jnp.concatenate([route_probs.reshape(assigned), jnp.zeros((1,), jnp.bfloat16)])[anchor]
    sent_p = sent_p.reshape(expert_count, capacity)
    gate_w = w_gate[0]
    up_w = w_up[0]
    down_w = w_down[0]
    recv_x, recv_dy, recv_p = (
        lax.all_to_all(sent_x, "expert", split_axis=0, concat_axis=0, tiled=True),
        lax.all_to_all(sent_dy, "expert", split_axis=0, concat_axis=0, tiled=True),
        lax.all_to_all(sent_p, "expert", split_axis=0, concat_axis=0, tiled=True),
    )
    x_rows = recv_x.reshape(rows_all, columns)
    dy_rows = recv_dy.reshape(rows_all, columns)
    gate_part = jnp.dot(x_rows, gate_w, preferred_element_type=jnp.float32)
    up_part = jnp.dot(x_rows, up_w, preferred_element_type=jnp.float32)
    cot_part = lax.dot_general(
        dy_rows, down_w, (((1,), (1,)), ((), ())), preferred_element_type=jnp.float32
    )
    gate_probs = recv_p.reshape(rows_all).astype(jnp.float32)
    gate_sum, up_sum, grad_h = (
        lax.psum(gate_part.astype(jnp.bfloat16), "dp").astype(jnp.float32),
        lax.psum(up_part.astype(jnp.bfloat16), "dp").astype(jnp.float32),
        lax.psum(cot_part.astype(jnp.bfloat16), "dp").astype(jnp.float32),
    )
    h_scaled, d_gate, d_up, prob_grad = local_step(gate_sum, up_sum, grad_h, gate_probs)
    dx_rows = lax.dot_general(
        d_gate, gate_w, (((1,), (1,)), ((), ())), preferred_element_type=jnp.float32
    ) + lax.dot_general(d_up, up_w, (((1,), (1,)), ((), ())), preferred_element_type=jnp.float32)
    dx_rows = dx_rows.astype(jnp.bfloat16)
    grad_gate = lax.dot_general(
        x_rows, d_gate, (((0,), (0,)), ((), ())), preferred_element_type=jnp.float32
    )
    grad_up = lax.dot_general(
        x_rows, d_up, (((0,), (0,)), ((), ())), preferred_element_type=jnp.float32
    )
    grad_down = lax.dot_general(
        h_scaled, dy_rows, (((0,), (0,)), ((), ())), preferred_element_type=jnp.float32
    )
    back_dx, back_p = (
        lax.all_to_all(
            dx_rows.reshape(expert_count, capacity, columns),
            "expert",
            split_axis=0,
            concat_axis=0,
            tiled=True,
        ),
        lax.all_to_all(
            prob_grad.reshape(expert_count, capacity),
            "expert",
            split_axis=0,
            concat_axis=0,
            tiled=True,
        ),
    )
    per_assign = (
        back_dx.reshape(rows_all, columns)[target]
        .astype(jnp.float32)
        .reshape(token_count, fanout, columns)
    )
    grad_tokens = jnp.sum(per_assign, axis=1).astype(jnp.bfloat16)
    d_probs = back_p.reshape(rows_all)[target].reshape(token_count, fanout)
    return (
        grad_tokens,
        grad_gate.astype(jnp.bfloat16)[None],
        grad_up.astype(jnp.bfloat16)[None],
        grad_down.astype(jnp.bfloat16)[None],
        d_probs,
    )


def solution(mesh):
    in_specs = (
        P("expert", "dp"),
        P("expert", "dp"),
        P("expert", None),
        P("expert", None),
        P("expert", "dp", None),
        P("expert", "dp", None),
        P("expert", None, "dp"),
    )
    out_specs = (
        P("expert", "dp"),
        P("expert", "dp", None),
        P("expert", "dp", None),
        P("expert", None, "dp"),
        P("expert", None),
    )
    return jax.shard_map(local, mesh=mesh, in_specs=in_specs, out_specs=out_specs, check_vma=False)
```

profile of v0, /device:TPU:1, one launch (start us, length us, event | category | flops | bytes accessed | tf_op | source)
XLA Modules:
  0.0 283.4 jit_solution(15510139026061400797)
XLA Ops:
  9.3 1.8 reduce-window.6
  11.6 3.4 %scatter_custom_fusion = s32[896]{0:T(1024)S(1)} fusion(s32[768]{0:T(1024)S(1)} %fusion.30, s32[768]{0:T(1024)S(1)} %iota.11, s32[]{:T(128)} %constant.8.clone.1), kind=kCustom, calls=%fused_computation.66 | custom fusion | bytes 3588 | tf_op jit(solution)/shard_map/scatter | solution.py:43
  15.9 3.5 %gather_fusion.2 = bf16[896,512]{1,0:T(8,128)(2,1)S(1)} fusion(bf16[129,512]{1,0:T(8,128)(2,1)S(1)} %concatenate.11, s32[1024]{0:T(1024)S(1)} %get-tuple-element.23), kind=kCustom, calls=%fused_computation.2 | custom fusion | bytes 1838592 | tf_op jit(solution)/shard_map/gather | solution.py:47
  20.7 14.8 %all-to-all-start.2 = ((bf16[64,14,512]{2,1,0:T(8,128)(2,1)}), bf16[64,14,512]{2,1,0:T(8,128)(2,1)S(1)}, u32[]{:S(2)}, u32[]{:S(2)}) async-start(bf16[64,14,512]{2,1,0:T(8,128)(2,1)} %reshape.118), calls=%async_computation.2 | async-start | bytes 2097152 | tf_op jit(solution)/shard_map/all_to_all | solution.py:59
  35.6 3.5 %gather_fusion.1 = bf16[896,512]{1,0:T(8,128)(2,1)S(1)} fusion(bf16[129,512]{1,0:T(8,128)(2,1)S(1)} %concatenate.10, s32[1024]{0:T(1024)S(1)} %get-tuple-element.23), kind=kCustom, calls=%fused_computation.1 | custom fusion | bytes 1838592 | tf_op jit(solution)/shard_map/gather | solution.py:50
  40.4 23.7 %all-to-all-done.2 = bf16[64,14,512]{2,1,0:T(8,128)(2,1)S(1)} async-done(((bf16[64,14,512]{2,1,0:T(8,128)(2,1)}), bf16[64,14,512]{2,1,0:T(8,128)(2,1)S(1)}, u32[]{:S(2)}, u32[]{:S(2)}) %all-to-all-start.2) | async-done | bytes 917536 | tf_op jit(solution)/shard_map/all_to_all | solution.py:59
  64.1 6.2 %all-to-all-start.1 = ((bf16[64,14,512]{2,1,0:T(8,128)(2,1)}), bf16[64,14,512]{2,1,0:T(8,128)(2,1)S(1)}, u32[]{:S(2)}, u32[]{:S(2)}) async-start(bf16[64,14,512]{2,1,0:T(8,128)(2,1)} %reshape.116), calls=%async_computation.1 | async-start | bytes 2097152 | tf_op jit(solution)/shard_map/all_to_all | solution.py:60
  71.6 3.3 %convolution_convert_fusion = bf16[896,768]{1,0:T(8,128)(2,1)} fusion(bf16[896,512]{1,0:T(8,128)(2,1)} %reshape.119, bf16[1,512,768]{2,1,0:T(8,128)(2,1)S(1)} %copy-done), kind=kOutput, calls=%fused_computation.27 | convolution fusion | flops 705331200 | bytes 3080192 | tf_op jit(solution)/shard_map/dot_general | solution.py:65
  74.9 2.0 convolution_convert_fusion.1
  76.9 22.0 %all-to-all-done.1 = bf16[64,14,512]{2,1,0:T(8,128)(2,1)S(1)} async-done(((bf16[64,14,512]{2,1,0:T(8,128)(2,1)}), bf16[64,14,512]{2,1,0:T(8,128)(2,1)S(1)}, u32[]{:S(2)}, u32[]{:S(2)}) %all-to-all-start.1) | async-done | bytes 917536 | tf_op jit(solution)/shard_map/all_to_all | solution.py:60
  99.1 3.4 %convolution_convert_fusion.2 = bf16[896,768]{1,0:T(8,128)(2,1)} fusion(bf16[896,512]{1,0:T(8,128)(2,1)S(1)} %reshape.117, bf16[1,768,512]{2,1,0:T(8,128)(2,1)} %param.13), kind=kOutput, calls=%fused_computation.29 | convolution fusion | flops 705331200 | bytes 3080192 | tf_op jit(solution)/shard_map/dot_general | solution.py:67
  103.5 5.8 %gather_fusion = bf16[896]{0:T(1024)(128)(2,1)S(1)} fusion(bf16[769]{0:T(1024)(128)(2,1)S(1)} %pad_maximum_fusion, s32[1024]{0:T(1024)S(1)} %get-tuple-element.24), kind=kCustom, calls=%fused_computation | custom fusion | bytes 7168 | tf_op jit(solution)/shard_map/gather | solution.py:53
  109.5 15.3 %all_to_all.31 = bf16[64,1,14]{2,1,0:T(2,128)(2,1)S(1)} all-to-all(bf16[64,1,14]{2,1,0:T(2,128)(2,1)S(1)} %all_to_all.25), channel_id=1, replica_groups=mesh['dp'=8,'expert'=64] {'expert'}, dimensions={0} | all-to-all | bytes 3584 | tf_op jit(solution)/shard_map/all_to_all | solution.py:61
  125.0 87.3 %all-reduce.5.cloned.1.call-done = (bf16[896,768]{1,0:T(8,128)(2,1)}, bf16[896,768]{1,0:T(8,128)(2,1)}, bf16[896,768]{1,0:T(8,128)(2,1)}) async-done(((bf16[896,768]{1,0:T(8,128)(2,1)}, bf16[896,768]{1,0:T(8,128)(2,1)}, bf16[896,768]{1,0:T(8,128)(2,1)}), (bf16[896,768]{1,0:T(8,128)(2,1)}, bf16[896,768]{1,0:T(8,128)(2,1)}, bf16[896,768]{1,0:T(8,128)(2,1)})) %all-reduce.5.cloned.1.call-update) | async-done | bytes 4128784 | tf_op jit(solution)/shard_map/psum | solution.py:73
  212.3 4.5 %fusion.1 = (bf16[896,768]{1,0:T(8,128)(2,1)}, bf16[896,768]{1,0:T(8,128)(2,1)S(1)}, bf16[896,768]{1,0:T(8,128)(2,1)S(1)}) fusion(bf16[896,768]{1,0:T(8,128)(2,1)} %get-tuple-element.16, f32[896]{0:T(1024)S(1)} %reshape.124, bf16[896,768]{1,0:T(8,128)(2,1)} %get-tuple-element.17, bf16[896,768]{1,0:T(8,128)(2,1)} %get-tuple-element.15), kind=kLoop, calls=%fused_computation.15 | loop fusion | flops 13074432 | bytes 8261120 | tf_op jit(solution)/shard_map/convert_element_type | solution.py:20
  218.1 11.4 %all-to-all-start.4 = ((bf16[64,1,14]{2,1,0:T(2,128)(2,1)}), bf16[64,1,14]{2,1,0:T(2,128)(2,1)}, u32[]{:S(2)}, u32[]{:S(2)}) async-start(bf16[64,1,14]{2,1,0:T(2,128)(2,1)} %convert_element_type.101), calls=%async_computation.4 | async-start | bytes 65536 | tf_op jit(solution)/shard_map/all_to_all | solution.py:98
  233.2 5.5 %all-to-all-done.4 = bf16[64,1,14]{2,1,0:T(2,128)(2,1)} async-done(((bf16[64,1,14]{2,1,0:T(2,128)(2,1)}), bf16[64,1,14]{2,1,0:T(2,128)(2,1)}, u32[]{:S(2)}, u32[]{:S(2)}) %all-to-all-start.4) | async-done | bytes 1824 | tf_op jit(solution)/shard_map/all_to_all | solution.py:98
  238.6 4.9 %all-to-all-start.3 = ((bf16[64,14,512]{2,1,0:T(8,128)(2,1)}), bf16[64,14,512]{2,1,0:T(8,128)(2,1)S(1)}, u32[]{:S(2)}, u32[]{:S(2)}) async-start(bf16[64,14,512]{2,1,0:T(8,128)(2,1)} %reshape.120), calls=%async_computation.3 | async-start | bytes 2097152 | tf_op jit(solution)/shard_map/all_to_all | solution.py:91
  243.5 3.7 %fusion.15 = bf16[1,512,768]{2,1,0:T(8,128)(2,1)} fusion(bf16[896,512]{1,0:T(8,128)(2,1)} %reshape.119, bf16[896,768]{1,0:T(8,128)(2,1)} %get-tuple-element.18), kind=kOutput, calls=%fused_computation.35 | convolution fusion | flops 705036288 | bytes 3080192 | tf_op jit(solution)/shard_map/dot_general | solution.py:84
  247.2 1.9 fusion.14
  249.1 2.0 fusion.16
  252.1 5.0 %gather_fusion.4 = bf16[768]{0:T(1024)(128)(2,1)S(1)} fusion(bf16[896]{0:T(1024)(128)(2,1)S(1)} %reshape.122, s32[1024]{0:T(1024)S(1)} %pad_clamp_fusion), kind=kCustom, calls=%fused_computation.4 | custom fusion | bytes 6144 | tf_op jit(solution)/shard_map/gather | solution.py:112
  258.0 14.0 %all-to-all-done.3 = bf16[64,14,512]{2,1,0:T(8,128)(2,1)S(1)} async-done(((bf16[64,14,512]{2,1,0:T(8,128)(2,1)}), bf16[64,14,512]{2,1,0:T(8,128)(2,1)S(1)}, u32[]{:S(2)}, u32[]{:S(2)}) %all-to-all-start.3) | async-done | bytes 917536 | tf_op jit(solution)/shard_map/all_to_all | solution.py:91
  272.3 2.7 gather_fusion.3
  (67 shorter events, 17.6 us)
Async XLA Ops:
  7.2 64.4 %copy-start = (bf16[1,512,768]{2,1,0:T(8,128)(2,1)S(1)}, bf16[1,512,768]{2,1,0:T(8,128)(2,1)}, u32[]{:S(2)}) copy-start(bf16[1,512,768]{2,1,0:T(8,128)(2,1)} %param.11) | copy-start | bytes 2359300
  19.4 16.1 %copy-start.9 = (bf16[128,512]{1,0:T(8,128)(2,1)S(1)}, bf16[128,512]{1,0:T(8,128)(2,1)}, u32[]{:S(2)}) copy-start(bf16[128,512]{1,0:T(8,128)(2,1)} %param.8) | copy-start | bytes 393220
  20.7 43.4 %all-to-all-start.2 = ((bf16[64,14,512]{2,1,0:T(8,128)(2,1)}), bf16[64,14,512]{2,1,0:T(8,128)(2,1)S(1)}, u32[]{:S(2)}, u32[]{:S(2)}) async-start(bf16[64,14,512]{2,1,0:T(8,128)(2,1)} %reshape.118), calls=%async_computation.2 | async-start | bytes 2097152 | tf_op jit(solution)/shard_map/all_to_all | solution.py:59
  64.1 34.7 %all-to-all-start.1 = ((bf16[64,14,512]{2,1,0:T(8,128)(2,1)}), bf16[64,14,512]{2,1,0:T(8,128)(2,1)S(1)}, u32[]{:S(2)}, u32[]{:S(2)}) async-start(bf16[64,14,512]{2,1,0:T(8,128)(2,1)} %reshape.116), calls=%async_computation.1 | async-start | bytes 2097152 | tf_op jit(solution)/shard_map/all_to_all | solution.py:60
  70.3 142.0 %all-reduce.5.cloned.1.call-start = ((), (), s32[]{:S(2)}) async-start(), calls=%async_computation.5 | async-start | bytes 8257536 | tf_op jit(solution)/shard_map/psum | solution.py:73
  71.6 3.3 %copy-start.5 = (bf16[896,512]{1,0:T(8,128)(2,1)S(1)}, bf16[896,512]{1,0:T(8,128)(2,1)}, u32[]{:S(2)}) copy-start(bf16[896,512]{1,0:T(8,128)(2,1)} %reshape.119) | copy-start | bytes 2752516
  71.6 3.3 %copy-start.11 = (bf16[1,512,768]{2,1,0:T(8,128)(2,1)S(1)}, bf16[1,512,768]{2,1,0:T(8,128)(2,1)}, u32[]{:S(2)}) copy-start(bf16[1,512,768]{2,1,0:T(8,128)(2,1)} %param.12) | copy-start | bytes 2359300
  99.1 3.5 %copy-start.7 = (bf16[896,512]{1,0:T(8,128)(2,1)}, bf16[896,512]{1,0:T(8,128)(2,1)S(1)}, u32[]{:S(2)}) copy-start(bf16[896,512]{1,0:T(8,128)(2,1)S(1)} %reshape.117) | copy-start | bytes 2752516
  102.6 0.7 copy-start.10
  212.3 4.5 %copy-start.1 = (bf16[896,768]{1,0:T(8,128)(2,1)S(1)}, bf16[896,768]{1,0:T(8,128)(2,1)}, u32[]{:S(2)}) copy-start(bf16[896,768]{1,0:T(8,128)(2,1)} %get-tuple-element.16) | copy-start | bytes 4128772
  216.8 13.6 %copy-start.2 = (bf16[896,768]{1,0:T(8,128)(2,1)}, bf16[896,768]{1,0:T(8,128)(2,1)S(1)}, u32[]{:S(2)}) copy-start(bf16[896,768]{1,0:T(8,128)(2,1)S(1)} %get-tuple-element.19) | copy-start | bytes 4128772
  218.1 20.6 %all-to-all-start.4 = ((bf16[64,1,14]{2,1,0:T(2,128)(2,1)}), bf16[64,1,14]{2,1,0:T(2,128)(2,1)}, u32[]{:S(2)}, u32[]{:S(2)}) async-start(bf16[64,1,14]{2,1,0:T(2,128)(2,1)} %convert_element_type.101), calls=%async_computation.4 | async-start | bytes 65536 | tf_op jit(solution)/shard_map/all_to_all | solution.py:98
  229.4 1.3 copy-start.4
  229.4 1.5 copy-start.12
  238.6 33.4 %all-to-all-start.3 = ((bf16[64,14,512]{2,1,0:T(8,128)(2,1)}), bf16[64,14,512]{2,1,0:T(8,128)(2,1)S(1)}, u32[]{:S(2)}, u32[]{:S(2)}) async-start(bf16[64,14,512]{2,1,0:T(8,128)(2,1)} %reshape.120), calls=%async_computation.3 | async-start | bytes 2097152 | tf_op jit(solution)/shard_map/all_to_all | solution.py:91
  243.5 3.7 %copy-start.3 = (bf16[896,768]{1,0:T(8,128)(2,1)S(1)}, bf16[896,768]{1,0:T(8,128)(2,1)}, u32[]{:S(2)}) copy-start(bf16[896,768]{1,0:T(8,128)(2,1)} %copy-done.2) | copy-start | bytes 4128772
  243.5 3.7 %copy-start.6 = (bf16[896,512]{1,0:T(8,128)(2,1)S(1)}, bf16[896,512]{1,0:T(8,128)(2,1)}, u32[]{:S(2)}) copy-start(bf16[896,512]{1,0:T(8,128)(2,1)} %reshape.119) | copy-start | bytes 2752516
  247.2 1.9 copy-start.8
Sparse Core Ops, SparseCore 0:
  102.7 109.5 all-reduce.4
where the time goes:
time: 284 us; the launch traced here: 283 us
  waiting for transfers between devices  152 us (54%)
  starting transfers between devices  37.3 us (13%)
  local copies, waits for them, and re-layouts  35.8 us (13%)
  matrix products  18.1 us (6%)
  blocking collectives  15.3 us (5%)
  between operations  14.3 us (5%)
  other arithmetic  10 us (4%)
    psum x1, waiting for transfers between devices, local(): lax.psum(up_part.astype(jnp.bfloat16), 'dp').astype(jnp.float32)  87.3 us
    all_to_all x1, waiting for transfers between devices, local(): lax.all_to_all(sent_x, 'expert', split_axis=0, concat_axis=0, tiled=True)  23.7 us
    all_to_all x1, waiting for transfers between devices, local(): lax.all_to_all(sent_dy, 'expert', split_axis=0, concat_axis=0, tiled=True)  22 us
    all_to_all x1, blocking collectives, local(): lax.all_to_all(sent_p, 'expert', split_axis=0, concat_axis=0, tiled=True)  15.3 us
    all_to_all x1, starting transfers between devices, local(): lax.all_to_all(sent_x, 'expert', split_axis=0, concat_axis=0, tiled=True)  14.8 us
    all_to_all x1, waiting for transfers between devices, local(): lax.all_to_all(dx_rows.reshape(expert_count, capacity, columns), 'expert'...  14 us
    all_to_all x1, starting transfers between devices, local(): lax.all_to_all(prob_grad.reshape(expert_count, capacity), 'expert', split...  11.4 us
    all_to_all x1, starting transfers between devices, local(): lax.all_to_all(sent_dy, 'expert', split_axis=0, concat_axis=0, tiled=True)  6.2 us
  transfers between devices with their start and end apart: 5, of which 5 were waited for; matrix products, arithmetic and copies ran while one was open for 12% of the time, Pallas kernels for 0%

commit v1 on v0

v1 whole, which is shorter than its diff:
```python
import jax
import jax.numpy as jnp
from jax import lax
from jax.sharding import PartitionSpec as P


def silu_parts(gate_sum):
    logistic = jax.nn.sigmoid(gate_sum)
    return (gate_sum * logistic, logistic * (1.0 + gate_sum * (1.0 - logistic)))


def local_step(gate_sum, up_sum, grad_h, gate_probs):
    activated, derivative = silu_parts(gate_sum)
    hidden_f = lax.optimization_barrier((activated * up_sum).astype(jnp.bfloat16)).astype(
        jnp.float32
    )
    prob_grad = jnp.sum(hidden_f * grad_h, axis=1).astype(jnp.bfloat16)
    scaled = gate_probs[:, None] * grad_h
    d_gate = (scaled * up_sum * derivative).astype(jnp.bfloat16)
    d_up = (scaled * activated).astype(jnp.bfloat16)
    h_scaled = (gate_probs[:, None] * hidden_f).astype(jnp.bfloat16)
    return (h_scaled, d_gate, d_up, prob_grad)


def contract_rows(a, b):
    return lax.dot_general(a, b, (((0,), (0,)), ((), ())), preferred_element_type=jnp.float32)


def contract_columns(a, b):
    return lax.dot_general(a, b, (((1,), (1,)), ((), ())), preferred_element_type=jnp.float32)


def exchange(rows):
    return lax.all_to_all(rows, "expert", split_axis=0, concat_axis=0, tiled=True)


def local(tokens, cotangent, expert_ids, route_probs, w_gate, w_up, w_down):
    expert_count = lax.axis_size("expert")
    token_count, columns = tokens.shape
    fanout = expert_ids.shape[1]
    capacity = max(2, 7 * token_count * fanout // (6 * expert_count))
    gate_w, up_w, down_w = w_gate[0], w_up[0], w_down[0]

    experts = jnp.arange(expert_count, dtype=jnp.int32)
    hits = expert_ids.T[:, None, :] == experts[None, :, None]
    chosen = jnp.any(hits, axis=0)
    order = jnp.arange(token_count, dtype=jnp.int32)
    before = (order[:, None] < order[None, :]).astype(jnp.bfloat16)
    earlier = jnp.dot(chosen.astype(jnp.bfloat16), before, preferred_element_type=jnp.float32)
    slot_of = jnp.where(chosen, earlier.astype(jnp.int32), -1)
    probs_f = route_probs.astype(jnp.float32)
    prob_of = jnp.sum(jnp.where(hits, probs_f.T[:, None, :], 0.0), axis=0)
    both = jnp.concatenate([tokens, cotangent], axis=1)

    chunks = ((0, 8), (8, capacity))
    ROWS = 8
    picks, received = [], []
    for first, last in chunks:
        slots = first + jnp.arange(ROWS, dtype=jnp.int32)
        wanted = jnp.where(slots < last, slots, -2)
        pick = (slot_of[:, None, :] == wanted[None, :, None]).astype(jnp.bfloat16)
        picks.append(pick.reshape(expert_count * ROWS, token_count))
    all_slots = jnp.arange(capacity, dtype=jnp.int32)
    sent_p = jnp.sum(
        jnp.where(slot_of[:, None, :] == all_slots[None, :, None], prob_of[:, None, :], 0.0), axis=2
    ).astype(jnp.bfloat16)
    p_row = jnp.pad(sent_p, ((0, 0), (0, 2 * columns - capacity)))
    for index, (first, last) in enumerate(chunks):
        rows = jnp.dot(picks[index], both, preferred_element_type=jnp.float32)
        rows = rows.astype(jnp.bfloat16).reshape(expert_count, ROWS, 2 * columns)
        if index == 1:
            row_id = jnp.arange(ROWS, dtype=jnp.int32)
            rows = jnp.where((row_id == ROWS - 1)[None, :, None], p_row[:, None, :], rows)
        if index == 1:
            rows, received[0] = lax.optimization_barrier((rows, received[0]))
        received.append(exchange(rows))
    recv_p = received[1][:, ROWS - 1, :capacity]

    parts = []
    for index, (first, last) in enumerate(chunks):
        got = received[index][:, : last - first].reshape(expert_count * (last - first), 2 * columns)
        x_rows, dy_rows = got[:, :columns], got[:, columns:]
        gate_part = jnp.dot(x_rows, gate_w, preferred_element_type=jnp.float32)
        up_part = jnp.dot(x_rows, up_w, preferred_element_type=jnp.float32)
        cot_part = contract_columns(dy_rows, down_w)
        sums = tuple(v.astype(jnp.bfloat16) for v in (gate_part, up_part, cot_part))
        parts.append((x_rows, dy_rows, sums))

    grads, backs, summed = [], [], None
    for index, (first, last) in enumerate(chunks):
        x_rows, dy_rows, sums = parts[index]
        if summed is not None:
            sums, summed = lax.optimization_barrier((sums, summed))
        reduced = tuple(lax.psum(v, "dp") for v in sums)
        summed = reduced
        parts[index] = (x_rows, dy_rows, reduced)
        if index == 1:
            pass
    for index, (first, last) in enumerate(chunks):
        x_rows, dy_rows, reduced = parts[index]
        count = last - first
        probs = recv_p[:, first:last].reshape(expert_count * count).astype(jnp.float32)
        gate_sum, up_sum, grad_h = (v.astype(jnp.float32) for v in reduced)
        h_scaled, d_gate, d_up, prob_grad = local_step(gate_sum, up_sum, grad_h, probs)
        dx_rows = contract_columns(d_gate, gate_w) + contract_columns(d_up, up_w)
        dx_rows = dx_rows.astype(jnp.bfloat16).reshape(expert_count, count, columns)
        prob_row = jnp.pad(prob_grad.reshape(expert_count, count), ((0, 0), (0, columns - count)))
        backs.append(exchange(jnp.concatenate([dx_rows, prob_row[:, None, :]], axis=1)))
        grads.append((contract_rows(x_rows, d_gate), contract_rows(x_rows, d_up),
                      contract_rows(h_scaled, dy_rows)))

    grad_gate, grad_up, grad_down = (a + b for a, b in zip(*grads))
    total = jnp.zeros((token_count, columns), jnp.float32)
    back_p = []
    for index, (first, last) in enumerate(chunks):
        count = last - first
        pick = picks[index].reshape(expert_count, ROWS, token_count)[:, :count]
        total += contract_rows(
            pick.reshape(expert_count * count, token_count),
            backs[index][:, :count].reshape(expert_count * count, columns),
        )
        back_p.append(backs[index][:, count, :count])
    back_p = jnp.concatenate(back_p, axis=1).astype(jnp.float32)
    back_of = jnp.sum(
        jnp.where(slot_of[:, None, :] == all_slots[None, :, None], back_p[:, :, None], 0.0), axis=1
    )
    d_probs = jnp.sum(jnp.where(hits, back_of[None], 0.0), axis=1).T.astype(jnp.bfloat16)
    return (
        total.astype(jnp.bfloat16),
        grad_gate.astype(jnp.bfloat16)[None],
        grad_up.astype(jnp.bfloat16)[None],
        grad_down.astype(jnp.bfloat16)[None],
        d_probs,
    )


def solution(mesh):
    in_specs = (
        P("expert", "dp"),
        P("expert", "dp"),
        P("expert", None),
        P("expert", None),
        P("expert", "dp", None),
        P("expert", "dp", None),
        P("expert", None, "dp"),
    )
    out_specs = (
        P("expert", "dp"),
        P("expert", "dp", None),
        P("expert", "dp", None),
        P("expert", None, "dp"),
        P("expert", None),
    )
    return jax.shard_map(local, mesh=mesh, in_specs=in_specs, out_specs=out_specs, check_vma=False)
```

time: 284 us -> 301 us (1.060)
  waiting for transfers between devices: 152 us -> 177 us
  local copies, waits for them, and re-layouts: 35.8 us -> 11.3 us
  matrix products: 18.1 us -> 35.6 us
  blocking collectives: 15.3 us -> 0 us
  starting transfers between devices: 37.3 us -> 51.4 us
    all_to_all x4, waiting for transfers between devices: 65.2 us -> 88 us  [exchange(): lax.all_to_all(rows, 'expert', split_axis=0, concat_axis=0, tiled=True)]
    gather x6 -> x0, local copies, waits for them, and re-layouts: 20.7 us -> none  [the longest x1 5.78 us: local(): jnp.concatenate([route_probs.reshape(assigned), jnp.zeros((1,), jnp.bfloa...]
    dot_general x6 -> x17, matrix products: 12.9 us -> 28.7 us  [the longest x8 14 us: contract_rows(): lax.dot_general(a, b, (((0,), (0,)), ((), ())), preferred_element_type=jn...]
    all_to_all x1 -> x0, blocking collectives: 15.3 us -> none  [local(): lax.all_to_all(sent_p, 'expert', split_axis=0, concat_axis=0, tiled=True)]
    all_to_all x4, starting transfers between devices: 37.3 us -> 51.3 us  [exchange(): lax.all_to_all(rows, 'expert', split_axis=0, concat_axis=0, tiled=True)]
    scatter x1 -> x0, local copies, waits for them, and re-layouts: 3.38 us -> none  [local(): anchor = jnp.full((rows_all,), assigned, jnp.int32).at[target].set(jnp.ar...]
    concatenate x1 -> x2, other arithmetic: 0.01 us -> 3.35 us  [local(): jnp.concatenate([dx_rows, prob_row[:, None, :]], axis=1)]
    psum x1 -> x2, waiting for transfers between devices: 87.3 us -> 89.3 us  [local(): reduced = tuple((lax.psum(v, 'dp') for v in sums))]
  transfers between devices with their start and end apart: 5 -> 6, of which waited for: 5 -> 6; matrix products, arithmetic and copies ran while one was open for 12% -> 9% of each run, Pallas kernels for 0% -> 0%
where the time goes in v1:
time: 301 us
  waiting for transfers between devices  177 us (59%)
  starting transfers between devices  51.4 us (17%)
  matrix products  35.6 us (12%)
  between operations  14.3 us (5%)
  local copies, waits for them, and re-layouts  11.3 us (4%)
  other arithmetic  10.6 us (4%)
    psum x2, waiting for transfers between devices, local(): reduced = tuple((lax.psum(v, 'dp') for v in sums))  89.3 us
    all_to_all x4, waiting for transfers between devices, exchange(): lax.all_to_all(rows, 'expert', split_axis=0, concat_axis=0, tiled=True)  88 us
    all_to_all x4, starting transfers between devices, exchange(): lax.all_to_all(rows, 'expert', split_axis=0, concat_axis=0, tiled=True)  51.3 us
    dot_general x8, matrix products, contract_rows(): lax.dot_general(a, b, (((0,), (0,)), ((), ())), preferred_element_type=jn...  14 us
    dot_general x6, matrix products, contract_columns(): lax.dot_general(a, b, (((1,), (1,)), ((), ())), preferred_element_type=jn...  11.6 us
  transfers between devices with their start and end apart: 6, of which 6 were waited for; matrix products, arithmetic and copies ran while one was open for 9% of the time, Pallas kernels for 0%

profile of v1, /device:TPU:1, one launch (start us, length us, event | category | flops | bytes accessed | tf_op | source)
XLA Modules:
  0.0 300.5 jit_solution(16764445388935199631)
XLA Ops:
  11.5 14.8 %all-to-all-start = ((bf16[64,8,1024]{2,1,0:T(8,128)(2,1)}), bf16[64,8,1024]{2,1,0:T(8,128)(2,1)S(1)}, u32[]{:S(2)}, u32[]{:S(2)}) async-start(bf16[64,8,1024]{2,1,0:T(8,128)(2,1)} %fusion.14), calls=%async_computation | async-start | bytes 2097152 | tf_op jit(solution)/shard_map/all_to_all | solution.py:34
  28.4 26.5 %all-to-all-done = bf16[64,8,1024]{2,1,0:T(8,128)(2,1)S(1)} async-done(((bf16[64,8,1024]{2,1,0:T(8,128)(2,1)}), bf16[64,8,1024]{2,1,0:T(8,128)(2,1)S(1)}, u32[]{:S(2)}, u32[]{:S(2)}) %all-to-all-start) | async-done | bytes 1048608 | tf_op jit(solution)/shard_map/all_to_all | solution.py:34
  54.9 6.2 %all-to-all-start.1 = ((bf16[64,8,1024]{2,1,0:T(8,128)(2,1)}), bf16[64,8,1024]{2,1,0:T(8,128)(2,1)S(1)}, u32[]{:S(2)}, u32[]{:S(2)}) async-start(bf16[64,8,1024]{2,1,0:T(8,128)(2,1)} %fusion.34), calls=%async_computation.1 | async-start | bytes 2097152 | tf_op jit(solution)/shard_map/all_to_all | solution.py:34
  65.7 24.0 %all-to-all-done.1 = bf16[64,8,1024]{2,1,0:T(8,128)(2,1)S(1)} async-done(((bf16[64,8,1024]{2,1,0:T(8,128)(2,1)}), bf16[64,8,1024]{2,1,0:T(8,128)(2,1)S(1)}, u32[]{:S(2)}, u32[]{:S(2)}) %all-to-all-start.1) | async-done | bytes 1048608 | tf_op jit(solution)/shard_map/all_to_all | solution.py:34
  91.1 2.7 convolution_convert_fusion.6
  96.4 55.5 %all-reduce.10.cloned.1.call-done = (bf16[512,768]{1,0:T(8,128)(2,1)}, bf16[512,768]{1,0:T(8,128)(2,1)}, bf16[512,768]{1,0:T(8,128)(2,1)}) async-done(((bf16[512,768]{1,0:T(8,128)(2,1)}, bf16[512,768]{1,0:T(8,128)(2,1)}, bf16[512,768]{1,0:T(8,128)(2,1)}), (bf16[512,768]{1,0:T(8,128)(2,1)}, bf16[512,768]{1,0:T(8,128)(2,1)}, bf16[512,768]{1,0:T(8,128)(2,1)})) %all-reduce.10.cloned.1.call-update) | async-done | bytes 2359312 | tf_op jit(solution)/shard_map/psum | solution.py:94
  151.9 2.7 fusion.3
  155.7 1.6 fusion.40
  157.4 2.7 fusion.20
  161.3 15.2 %all-to-all-start.2 = ((bf16[64,9,512]{2,1,0:T(8,128)(2,1)}), bf16[64,9,512]{2,1,0:T(8,128)(2,1)}, u32[]{:S(2)}, u32[]{:S(2)}) async-start(bf16[64,9,512]{2,1,0:T(8,128)(2,1)} %pad_maximum_fusion), calls=%async_computation.2 | async-start | bytes 2097152 | tf_op jit(solution)/shard_map/all_to_all | solution.py:34
  176.7 28.2 %all-to-all-done.2 = bf16[64,9,512]{2,1,0:T(8,128)(2,1)} async-done(((bf16[64,9,512]{2,1,0:T(8,128)(2,1)}), bf16[64,9,512]{2,1,0:T(8,128)(2,1)}, u32[]{:S(2)}, u32[]{:S(2)}) %all-to-all-start.2) | async-done | bytes 589856 | tf_op jit(solution)/shard_map/all_to_all | solution.py:34
  208.0 33.8 %all-reduce.8.cloned.1.call-done = (bf16[384,768]{1,0:T(8,128)(2,1)}, bf16[384,768]{1,0:T(8,128)(2,1)}, bf16[384,768]{1,0:T(8,128)(2,1)}) async-done(((bf16[384,768]{1,0:T(8,128)(2,1)}, bf16[384,768]{1,0:T(8,128)(2,1)}, bf16[384,768]{1,0:T(8,128)(2,1)}), (bf16[384,768]{1,0:T(8,128)(2,1)}, bf16[384,768]{1,0:T(8,128)(2,1)}, bf16[384,768]{1,0:T(8,128)(2,1)})) %all-reduce.8.cloned.1.call-update) | async-done | bytes 1769488 | tf_op jit(solution)/shard_map/psum | solution.py:94
  241.8 2.2 fusion.23
  244.3 1.8 fusion.50
  247.5 1.8 fusion.67
  250.2 3.1 %fusion.19 = bf16[384,512]{1,0:T(8,128)(2,1)} fusion(f32[384,512]{1,0:T(8,128)} %fusion.37, bf16[1,512,768]{2,1,0:T(8,128)(2,1)} %param.12, bf16[384,768]{1,0:T(8,128)(2,1)} %get-tuple-element.15, f32[384]{0:T(512)S(1)} %reshape.105, bf16[384,768]{1,0:T(8,128)(2,1)} %get-tuple-element.17), kind=kOutput, calls=%fused_computation.48 | convolution fusion | flops 305037312 | bytes 3147264 | tf_op jit(solution)/shard_map/dot_general | solution.py:30
  253.3 1.9 reshape.103
  255.2 2.2 pad_maximum_fusion.1
  257.4 15.1 %all-to-all-start.3 = ((bf16[64,7,512]{2,1,0:T(8,128)(2,1)}), bf16[64,7,512]{2,1,0:T(8,128)(2,1)}, u32[]{:S(2)}, u32[]{:S(2)}) async-start(bf16[64,7,512]{2,1,0:T(8,128)(2,1)} %pad_maximum_fusion.1), calls=%async_computation.3 | async-start | bytes 1048576 | tf_op jit(solution)/shard_map/all_to_all | solution.py:34
  272.6 3.1 %fusion.17 = bf16[1,768,512]{2,1,0:T(8,128)(2,1)} fusion(f32[768,512]{1,0:T(8,128)} %fusion.50, bf16[512,768]{1,0:T(8,128)(2,1)S(1)} %get-tuple-element.22, f32[512]{0:T(512)S(1)} %reshape.104, bf16[512,1024]{1,0:T(8,128)(2,1)S(1)} %bitcast.77), kind=kOutput, calls=%fused_computation.45 | convolution fusion | flops 404619264 | bytes 3672064 | tf_op jit(solution)/shard_map/dot_general | solution.py:26
  275.7 1.5 fusion.15
  278.6 1.8 fusion.16
  280.4 9.4 %all-to-all-done.3 = bf16[64,7,512]{2,1,0:T(8,128)(2,1)} async-done(((bf16[64,7,512]{2,1,0:T(8,128)(2,1)}), bf16[64,7,512]{2,1,0:T(8,128)(2,1)}, u32[]{:S(2)}, u32[]{:S(2)}) %all-to-all-start.3) | async-done | bytes 458784 | tf_op jit(solution)/shard_map/all_to_all | solution.py:34
  291.6 2.0 fusion.33
  (92 shorter events, 26.4 us)
Async XLA Ops:
  7.2 54.0 %copy-start = (bf16[1,512,768]{2,1,0:T(8,128)(2,1)S(1)}, bf16[1,512,768]{2,1,0:T(8,128)(2,1)}, u32[]{:S(2)}) copy-start(bf16[1,512,768]{2,1,0:T(8,128)(2,1)} %param.11) | copy-start | bytes 2359300
  10.1 16.3 %copy-start.14 = (bf16[128,6]{0,1:T(8,128)(2,1)S(1)}, bf16[128,6]{0,1:T(8,128)(2,1)}, u32[]{:S(2)}) copy-start(bf16[128,6]{0,1:T(8,128)(2,1)} %param.10) | copy-start | bytes 4612
  10.1 16.3 %copy-start.13 = (s32[128,6]{0,1:T(8,128)S(1)}, s32[128,6]{0,1:T(8,128)}, u32[]{:S(2)}) copy-start(s32[128,6]{0,1:T(8,128)} %param.9) | copy-start | bytes 9220
  11.5 43.4 %all-to-all-start = ((bf16[64,8,1024]{2,1,0:T(8,128)(2,1)}), bf16[64,8,1024]{2,1,0:T(8,128)(2,1)S(1)}, u32[]{:S(2)}, u32[]{:S(2)}) async-start(bf16[64,8,1024]{2,1,0:T(8,128)(2,1)} %fusion.14), calls=%async_computation | async-start | bytes 2097152 | tf_op jit(solution)/shard_map/all_to_all | solution.py:34
  54.9 34.7 %all-to-all-start.1 = ((bf16[64,8,1024]{2,1,0:T(8,128)(2,1)}), bf16[64,8,1024]{2,1,0:T(8,128)(2,1)S(1)}, u32[]{:S(2)}, u32[]{:S(2)}) async-start(bf16[64,8,1024]{2,1,0:T(8,128)(2,1)} %fusion.34), calls=%async_computation.1 | async-start | bytes 2097152 | tf_op jit(solution)/shard_map/all_to_all | solution.py:34
  61.1 90.8 %all-reduce.10.cloned.1.call-start = ((), (), s32[]{:S(2)}) async-start(), calls=%async_computation.5 | async-start | bytes 4718592 | tf_op jit(solution)/shard_map/psum | solution.py:94
  61.1 1.5 copy-start.17
  62.6 1.5 copy-start.15
  65.6 176.2 %all-reduce.8.cloned.1.call-start = ((), (), s32[]{:S(2)}) async-start(), calls=%async_computation.4 | async-start | bytes 3538944 | tf_op jit(solution)/shard_map/psum | solution.py:94
  91.1 2.7 copy-start.4
  91.1 2.7 copy-start.16
  151.9 2.7 copy-start.2
  157.3 2.7 copy-start.12
  161.3 43.6 %all-to-all-start.2 = ((bf16[64,9,512]{2,1,0:T(8,128)(2,1)}), bf16[64,9,512]{2,1,0:T(8,128)(2,1)}, u32[]{:S(2)}, u32[]{:S(2)}) async-start(bf16[64,9,512]{2,1,0:T(8,128)(2,1)} %pad_maximum_fusion), calls=%async_computation.2 | async-start | bytes 2097152 | tf_op jit(solution)/shard_map/all_to_all | solution.py:34
  241.8 2.2 copy-start.7
  241.8 2.5 copy-start.5
  257.4 32.4 %all-to-all-start.3 = ((bf16[64,7,512]{2,1,0:T(8,128)(2,1)}), bf16[64,7,512]{2,1,0:T(8,128)(2,1)}, u32[]{:S(2)}, u32[]{:S(2)}) async-start(bf16[64,7,512]{2,1,0:T(8,128)(2,1)} %pad_maximum_fusion.1), calls=%async_computation.3 | async-start | bytes 1048576 | tf_op jit(solution)/shard_map/all_to_all | solution.py:34
  272.6 3.1 %copy-start.1 = (f32[512,768]{1,0:T(8,128)S(1)}, f32[512,768]{1,0:T(8,128)}, u32[]{:S(2)}) copy-start(f32[512,768]{1,0:T(8,128)} %fusion.67) | copy-start | bytes 4718596
  275.7 1.5 copy-start.6
  275.7 1.5 copy-start.8
  275.7 1.5 copy-start.11
  277.2 1.1 copy-start.3
  277.2 1.4 copy-start.10
  278.6 13.1 %copy-start.9 = (f32[128,512]{1,0:T(8,128)S(1)}, f32[128,512]{1,0:T(8,128)}, u32[]{:S(2)}) copy-start(f32[128,512]{1,0:T(8,128)} %convolution_bitcast_fusion.1) | copy-start | bytes 786436
Sparse Core Ops, SparseCore 0:
  65.7 86.1 all-reduce.9
  157.5 84.3 all-reduce.7

commit v2 on v1

v2 whole, which is shorter than its diff:
```python
import jax
import jax.numpy as jnp
from jax import lax
from jax.sharding import PartitionSpec as P


def silu_parts(gate_sum):
    logistic = jax.nn.sigmoid(gate_sum)
    return (gate_sum * logistic, logistic * (1.0 + gate_sum * (1.0 - logistic)))


def local_step(gate_sum, up_sum, grad_h, gate_probs):
    activated, derivative = silu_parts(gate_sum)
    hidden_f = lax.optimization_barrier((activated * up_sum).astype(jnp.bfloat16)).astype(
        jnp.float32
    )
    prob_grad = jnp.sum(hidden_f * grad_h, axis=1).astype(jnp.bfloat16)
    scaled = gate_probs[:, None] * grad_h
    d_gate = (scaled * up_sum * derivative).astype(jnp.bfloat16)
    d_up = (scaled * activated).astype(jnp.bfloat16)
    h_scaled = (gate_probs[:, None] * hidden_f).astype(jnp.bfloat16)
    return (h_scaled, d_gate, d_up, prob_grad)


def contract_rows(a, b):
    return lax.dot_general(a, b, (((0,), (0,)), ((), ())), preferred_element_type=jnp.float32)


def contract_columns(a, b):
    return lax.dot_general(a, b, (((1,), (1,)), ((), ())), preferred_element_type=jnp.float32)


def exchange(rows):
    return lax.all_to_all(rows, "expert", split_axis=0, concat_axis=0, tiled=True)


def local(tokens, cotangent, expert_ids, route_probs, w_gate, w_up, w_down):
    expert_count = lax.axis_size("expert")
    token_count, columns = tokens.shape
    fanout = expert_ids.shape[1]
    capacity = max(2, 7 * token_count * fanout // (6 * expert_count))
    gate_w, up_w, down_w = w_gate[0], w_up[0], w_down[0]

    experts = jnp.arange(expert_count, dtype=jnp.int32)
    hits = expert_ids.T[:, None, :] == experts[None, :, None]
    chosen = jnp.any(hits, axis=0)
    order = jnp.arange(token_count, dtype=jnp.int32)
    before = (order[:, None] < order[None, :]).astype(jnp.bfloat16)
    earlier = jnp.dot(chosen.astype(jnp.bfloat16), before, preferred_element_type=jnp.float32)
    slot_of = jnp.where(chosen, earlier.astype(jnp.int32), -1)
    probs_f = route_probs.astype(jnp.float32)
    prob_of = jnp.sum(jnp.where(hits, probs_f.T[:, None, :], 0.0), axis=0)
    both = jnp.concatenate([tokens, cotangent], axis=1)

    all_slots = jnp.arange(capacity, dtype=jnp.int32)
    match = slot_of[:, None, :] == all_slots[None, :, None]
    padded = jnp.arange(capacity + 2, dtype=jnp.int32)
    pick = (slot_of[:, None, :] == padded[None, :, None]).astype(jnp.bfloat16)
    rows = jnp.dot(
        pick.reshape(expert_count * (capacity + 2), token_count),
        both,
        preferred_element_type=jnp.float32,
    ).astype(jnp.bfloat16).reshape(expert_count, capacity + 2, 2 * columns)
    sent_p = jnp.sum(jnp.where(match, prob_of[:, None, :], 0.0), axis=2).astype(jnp.bfloat16)
    p_row = jnp.pad(sent_p, ((0, 0), (0, 2 * columns - capacity)))
    rows = jnp.where((padded == capacity)[None, :, None], p_row[:, None, :], rows)
    received = exchange(rows)
    rows_all = expert_count * capacity
    gate_probs = received[:, capacity, :capacity].reshape(rows_all).astype(jnp.float32)
    got = received[:, :capacity].reshape(rows_all, 2 * columns)
    x_rows, dy_rows = got[:, :columns], got[:, columns:]
    parts = (
        jnp.dot(x_rows, gate_w, preferred_element_type=jnp.float32),
        jnp.dot(x_rows, up_w, preferred_element_type=jnp.float32),
        contract_columns(dy_rows, down_w),
    )
    gate_sum, up_sum, grad_h = (
        lax.psum(v.astype(jnp.bfloat16), "dp").astype(jnp.float32) for v in parts
    )
    h_scaled, d_gate, d_up, prob_grad = local_step(gate_sum, up_sum, grad_h, gate_probs)
    dx_rows = contract_columns(d_gate, gate_w) + contract_columns(d_up, up_w)
    dx_rows = dx_rows.astype(jnp.bfloat16).reshape(expert_count, capacity, columns)
    prob_row = jnp.pad(
        prob_grad.reshape(expert_count, capacity), ((0, 0), (0, columns - capacity))
    )
    back = exchange(jnp.concatenate([dx_rows, prob_row[:, None, :]], axis=1))
    grad_gate = contract_rows(x_rows, d_gate)
    grad_up = contract_rows(x_rows, d_up)
    grad_down = contract_rows(h_scaled, dy_rows)
    total = contract_rows(
        match.astype(jnp.bfloat16).reshape(rows_all, token_count),
        back[:, :capacity].reshape(rows_all, columns),
    )
    back_p = back[:, capacity, :capacity].astype(jnp.float32)
    back_of = jnp.sum(jnp.where(match, back_p[:, :, None], 0.0), axis=1)
    d_probs = jnp.sum(jnp.where(hits, back_of[None], 0.0), axis=1).T.astype(jnp.bfloat16)
    return (
        total.astype(jnp.bfloat16),
        grad_gate.astype(jnp.bfloat16)[None],
        grad_up.astype(jnp.bfloat16)[None],
        grad_down.astype(jnp.bfloat16)[None],
        d_probs,
    )


def solution(mesh):
    in_specs = (
        P("expert", "dp"),
        P("expert", "dp"),
        P("expert", None),
        P("expert", None),
        P("expert", "dp", None),
        P("expert", "dp", None),
        P("expert", None, "dp"),
    )
    out_specs = (
        P("expert", "dp"),
        P("expert", "dp", None),
        P("expert", "dp", None),
        P("expert", None, "dp"),
        P("expert", None),
    )
    return jax.shard_map(local, mesh=mesh, in_specs=in_specs, out_specs=out_specs, check_vma=False)
```

time: 301 us -> 262 us (0.87)
  blocking collectives: 0 us -> 65.8 us
  waiting for transfers between devices: 177 us -> 130 us
  starting transfers between devices: 51.4 us -> 11.6 us
  matrix products: 35.6 us -> 22.2 us
  local copies, waits for them, and re-layouts: 11.3 us -> 5.61 us
    all_to_all x4 -> x1, waiting for transfers between devices: 88 us -> 21.2 us  [exchange(): lax.all_to_all(rows, 'expert', split_axis=0, concat_axis=0, tiled=True)]
    all_to_all x0 -> x1, blocking collectives: none -> 65.8 us  [exchange(): lax.all_to_all(rows, 'expert', split_axis=0, concat_axis=0, tiled=True)]
    all_to_all x4 -> x1, starting transfers between devices: 51.3 us -> 11.5 us  [exchange(): lax.all_to_all(rows, 'expert', split_axis=0, concat_axis=0, tiled=True)]
    psum x2 -> x1, waiting for transfers between devices: 89.3 us -> 109 us  [local(): lax.psum(v.astype(jnp.bfloat16), 'dp').astype(jnp.float32)]
    dot_general x6 -> x3, matrix products: 11.6 us -> 4.76 us  [contract_columns(): lax.dot_general(a, b, (((1,), (1,)), ((), ())), preferred_element_type=jn...]
    dot_general x8 -> x4, matrix products: 14 us -> 10.2 us  [contract_rows(): lax.dot_general(a, b, (((0,), (0,)), ((), ())), preferred_element_type=jn...]
    dot_general x6 -> x3, matrix products: 9.84 us -> 7.05 us  [the longest x1 3.35 us: local(): jnp.dot(x_rows, gate_w, preferred_element_type=jnp.float32)]
  transfers between devices with their start and end apart: 6 -> 2, of which waited for: 6 -> 2; matrix products, arithmetic and copies ran while one was open for 9% -> 3% of each run, Pallas kernels for 0% -> 0%
where the time goes in v2:
time: 262 us; the launch traced here: 261 us
  waiting for transfers between devices  130 us (50%)
  blocking collectives  65.8 us (25%)
  matrix products  22.2 us (8%)
  between operations  14.2 us (5%)
  starting transfers between devices  11.6 us (4%)
  other arithmetic  11.5 us (4%)
  local copies, waits for them, and re-layouts  5.61 us (2%)
    psum x1, waiting for transfers between devices, local(): lax.psum(v.astype(jnp.bfloat16), 'dp').astype(jnp.float32)  109 us
    all_to_all x1, blocking collectives, exchange(): lax.all_to_all(rows, 'expert', split_axis=0, concat_axis=0, tiled=True)  65.8 us
    all_to_all x1, waiting for transfers between devices, exchange(): lax.all_to_all(rows, 'expert', split_axis=0, concat_axis=0, tiled=True)  21.2 us
    all_to_all x1, starting transfers between devices, exchange(): lax.all_to_all(rows, 'expert', split_axis=0, concat_axis=0, tiled=True)  11.5 us
    dot_general x4, matrix products, contract_rows(): lax.dot_general(a, b, (((0,), (0,)), ((), ())), preferred_element_type=jn...  10.2 us
  transfers between devices with their start and end apart: 2, of which 2 were waited for; matrix products, arithmetic and copies ran while one was open for 3% of the time, Pallas kernels for 0%

profile of v2, /device:TPU:1, one launch (start us, length us, event | category | flops | bytes accessed | tf_op | source)
XLA Modules:
  0.0 261.2 jit_solution(15965414682091480196)
XLA Ops:
  7.2 0.7 convert_bitcast_fusion
  8.8 0.7 select_reduce_fusion.3
  10.2 1.7 convolution_convert_fusion
  12.1 65.8 %all_to_all.10 = bf16[64,16,1024]{2,1,0:T(8,128)(2,1)S(1)} all-to-all(bf16[64,16,1024]{2,1,0:T(8,128)(2,1)S(1)} %broadcast_select_fusion), channel_id=1, replica_groups=mesh['dp'=8,'expert'=64] {'expert'}, dimensions={0} | all-to-all | bytes 4194304 | tf_op jit(solution)/shard_map/all_to_all | solution.py:34
  78.0 1.5 reshape.52
  79.5 3.4 %convolution_convert_fusion.1 = bf16[896,768]{1,0:T(8,128)(2,1)} fusion(bf16[1,512,768]{2,1,0:T(8,128)(2,1)S(1)} %copy-done, bf16[896,1024]{1,0:T(8,128)(2,1)} %reshape.52), kind=kOutput, calls=%fused_computation.23 | convolution fusion | flops 705331200 | bytes 3080192 | tf_op jit(solution)/shard_map/dot_general | solution.py:73
  82.9 2.0 convolution_convert_fusion.2
  84.9 2.0 convolution_convert_fusion.3
  87.2 109.1 %all-reduce.5.cloned.1.call-done = (bf16[896,768]{1,0:T(8,128)(2,1)}, bf16[896,768]{1,0:T(8,128)(2,1)}, bf16[896,768]{1,0:T(8,128)(2,1)}) async-done(((bf16[896,768]{1,0:T(8,128)(2,1)}, bf16[896,768]{1,0:T(8,128)(2,1)}, bf16[896,768]{1,0:T(8,128)(2,1)}), (bf16[896,768]{1,0:T(8,128)(2,1)}, bf16[896,768]{1,0:T(8,128)(2,1)}, bf16[896,768]{1,0:T(8,128)(2,1)})) %all-reduce.5.cloned.1.call-update) | async-done | bytes 4128784 | tf_op jit(solution)/shard_map/psum | solution.py:78
  196.3 4.5 %fusion.1 = (bf16[896,768]{1,0:T(8,128)(2,1)}, bf16[896,768]{1,0:T(8,128)(2,1)S(1)}, bf16[896,768]{1,0:T(8,128)(2,1)S(1)}) fusion(bf16[896,768]{1,0:T(8,128)(2,1)} %get-tuple-element.5, f32[896]{0:T(1024)S(1)} %reshape.54, bf16[896,768]{1,0:T(8,128)(2,1)} %get-tuple-element.7, bf16[896,768]{1,0:T(8,128)(2,1)} %get-tuple-element.6), kind=kLoop, calls=%fused_computation.9 | loop fusion | flops 13074432 | bytes 8261120 | tf_op jit(solution)/shard_map/convert_element_type | solution.py:20
  200.8 1.0 fusion.5
  201.8 0.8 convert_element_type.116
  202.7 0.8 copy.24
  203.4 0.9 fusion.24
  205.0 1.8 add_convert_fusion
  206.8 1.4 reshape.53
  208.2 1.3 pad_maximum_fusion
  209.5 11.5 %all-to-all-start.1 = ((bf16[64,15,512]{2,1,0:T(8,128)(2,1)}), bf16[64,15,512]{2,1,0:T(8,128)(2,1)}, u32[]{:S(2)}, u32[]{:S(2)}) async-start(bf16[64,15,512]{2,1,0:T(8,128)(2,1)} %pad_maximum_fusion), calls=%async_computation.1 | async-start | bytes 2097152 | tf_op jit(solution)/shard_map/all_to_all | solution.py:34
  221.1 3.2 %fusion.15 = bf16[1,512,768]{2,1,0:T(8,128)(2,1)} fusion(bf16[896,768]{1,0:T(8,128)(2,1)S(1)} %copy-done.7, bf16[896,1024]{1,0:T(8,128)(2,1)} %reshape.52), kind=kOutput, calls=%fused_computation.31 | convolution fusion | flops 705036288 | bytes 3080192 | tf_op jit(solution)/shard_map/dot_general | solution.py:26
  224.3 1.9 fusion.14
  226.3 2.0 fusion.16
  228.3 21.2 %all-to-all-done.1 = bf16[64,15,512]{2,1,0:T(8,128)(2,1)} async-done(((bf16[64,15,512]{2,1,0:T(8,128)(2,1)}), bf16[64,15,512]{2,1,0:T(8,128)(2,1)}, u32[]{:S(2)}, u32[]{:S(2)}) %all-to-all-start.1) | async-done | bytes 983072 | tf_op jit(solution)/shard_map/all_to_all | solution.py:34
  249.5 0.9 slice_convert_fusion
  250.7 3.0 %fusion.19 = bf16[128,512]{1,0:T(8,128)(2,1)} fusion(bf16[64,14,512]{2,1,0:T(8,128)(2,1)} %bitcast.42, s32[64,128]{1,0:T(8,128)S(1)} %copy-done.10), kind=kOutput, calls=%fused_computation.34 | convolution fusion | flops 117620736 | bytes 1081344 | tf_op jit(solution)/shard_map/dot_general | solution.py:26
  (52 shorter events, 3.6 us)
Async XLA Ops:
  7.2 72.3 %copy-start = (bf16[1,512,768]{2,1,0:T(8,128)(2,1)S(1)}, bf16[1,512,768]{2,1,0:T(8,128)(2,1)}, u32[]{:S(2)}) copy-start(bf16[1,512,768]{2,1,0:T(8,128)(2,1)} %param.11) | copy-start | bytes 2359300
  7.2 189.1 %all-reduce.5.cloned.1.call-start = ((), (), s32[]{:S(2)}) async-start(), calls=%async_computation.2 | async-start | bytes 8257536 | tf_op jit(solution)/shard_map/psum | solution.py:78
  8.8 3.0 %copy-start.9 = (s32[64,128]{1,0:T(8,128)}, s32[64,128]{1,0:T(8,128)S(1)}, u32[]{:S(2)}) copy-start(s32[64,128]{1,0:T(8,128)S(1)} %fusion.20) | copy-start | bytes 98308
  79.5 3.4 %copy-start.2 = (bf16[896,1024]{1,0:T(8,128)(2,1)S(1)}, bf16[896,1024]{1,0:T(8,128)(2,1)}, u32[]{:S(2)}) copy-start(bf16[896,1024]{1,0:T(8,128)(2,1)} %reshape.52) | copy-start | bytes 5505028
  79.5 3.4 %copy-start.15 = (bf16[1,512,768]{2,1,0:T(8,128)(2,1)S(1)}, bf16[1,512,768]{2,1,0:T(8,128)(2,1)}, u32[]{:S(2)}) copy-start(bf16[1,512,768]{2,1,0:T(8,128)(2,1)} %param.12) | copy-start | bytes 2359300
  82.9 2.0 copy-start.14
  87.2 113.6 %copy-start.12 = (f32[896]{0:T(1024)}, f32[896]{0:T(1024)S(1)}, u32[]{:S(2)}) copy-start(f32[896]{0:T(1024)S(1)} %reshape.54) | copy-start | bytes 10756
  196.3 4.5 %copy-start.1 = (bf16[896,768]{1,0:T(8,128)(2,1)S(1)}, bf16[896,768]{1,0:T(8,128)(2,1)}, u32[]{:S(2)}) copy-start(bf16[896,768]{1,0:T(8,128)(2,1)} %get-tuple-element.5) | copy-start | bytes 4128772
  200.8 3.5 %copy-start.4 = (bf16[896,768]{1,0:T(8,128)(2,1)}, bf16[896,768]{1,0:T(8,128)(2,1)S(1)}, u32[]{:S(2)}) copy-start(bf16[896,768]{1,0:T(8,128)(2,1)S(1)} %get-tuple-element.9) | copy-start | bytes 4128772
  203.4 1.3 copy-start.6
  203.4 1.5 copy-start.16
  206.8 1.4 copy-start.8
  209.5 11.5 %copy-start.7 = (bf16[896,768]{1,0:T(8,128)(2,1)S(1)}, bf16[896,768]{1,0:T(8,128)(2,1)}, u32[]{:S(2)}) copy-start(bf16[896,768]{1,0:T(8,128)(2,1)} %get-tuple-element.8) | copy-start | bytes 4128772
  209.5 40.0 %all-to-all-start.1 = ((bf16[64,15,512]{2,1,0:T(8,128)(2,1)}), bf16[64,15,512]{2,1,0:T(8,128)(2,1)}, u32[]{:S(2)}, u32[]{:S(2)}) async-start(bf16[64,15,512]{2,1,0:T(8,128)(2,1)} %pad_maximum_fusion), calls=%async_computation.1 | async-start | bytes 2097152 | tf_op jit(solution)/shard_map/all_to_all | solution.py:34
  221.1 3.3 %copy-start.3 = (bf16[896,1024]{1,0:T(8,128)(2,1)S(1)}, bf16[896,1024]{1,0:T(8,128)(2,1)}, u32[]{:S(2)}) copy-start(bf16[896,1024]{1,0:T(8,128)(2,1)} %reshape.52) | copy-start | bytes 5505028
  221.1 3.3 %copy-start.5 = (bf16[896,768]{1,0:T(8,128)(2,1)S(1)}, bf16[896,768]{1,0:T(8,128)(2,1)}, u32[]{:S(2)}) copy-start(bf16[896,768]{1,0:T(8,128)(2,1)} %copy-done.4) | copy-start | bytes 4128772
  224.3 1.9 copy-start.13
  226.3 24.2 %copy-start.10 = (s32[64,128]{1,0:T(8,128)S(1)}, s32[64,128]{1,0:T(8,128)}, u32[]{:S(2)}) copy-start(s32[64,128]{1,0:T(8,128)} %copy-done.9) | copy-start | bytes 98308
  226.3 27.5 %copy-start.11 = (s32[128,6]{0,1:T(8,128)S(1)}, s32[128,6]{0,1:T(8,128)}, u32[]{:S(2)}) copy-start(s32[128,6]{0,1:T(8,128)} %param.9) | copy-start | bytes 9220
Sparse Core Ops, SparseCore 0:
  87.0 109.2 all-reduce.4

commit v3 on v2

--- a/solution.py
+++ b/solution.py
@@ -34,6 +34,16 @@
     return lax.all_to_all(rows, "expert", split_axis=0, concat_axis=0, tiled=True)
 
 
+def sum_by_exchange(part, others):
+    count = lax.axis_size("dp")
+    slices = part.reshape(count, part.shape[0] // count, part.shape[1])
+    slices = lax.all_to_all(slices, "dp", split_axis=0, concat_axis=0, tiled=True)
+    total = jnp.sum(slices.astype(jnp.float32), axis=0).astype(jnp.bfloat16)
+    total, others = lax.optimization_barrier((total, others))
+    copies = jnp.broadcast_to(total[None], slices.shape)
+    return lax.all_to_all(copies, "dp", split_axis=0, concat_axis=0, tiled=True).reshape(part.shape), others
+
+
 def local(tokens, cotangent, expert_ids, route_probs, w_gate, w_up, w_down):
     expert_count = lax.axis_size("expert")
     token_count, columns = tokens.shape
@@ -50,33 +60,35 @@
     slot_of = jnp.where(chosen, earlier.astype(jnp.int32), -1)
     probs_f = route_probs.astype(jnp.float32)
     prob_of = jnp.sum(jnp.where(hits, probs_f.T[:, None, :], 0.0), axis=0)
-    both = jnp.concatenate([tokens, cotangent], axis=1)
 
     all_slots = jnp.arange(capacity, dtype=jnp.int32)
     match = slot_of[:, None, :] == all_slots[None, :, None]
     padded = jnp.arange(capacity + 2, dtype=jnp.int32)
     pick = (slot_of[:, None, :] == padded[None, :, None]).astype(jnp.bfloat16)
-    rows = jnp.dot(
-        pick.reshape(expert_count * (capacity + 2), token_count),
-        both,
-        preferred_element_type=jnp.float32,
-    ).astype(jnp.bfloat16).reshape(expert_count, capacity + 2, 2 * columns)
+    pick = pick.reshape(expert_count * (capacity + 2), token_count)
+
+    def rows_of(source):
+        rows = jnp.dot(pick, source, preferred_element_type=jnp.float32).astype(jnp.bfloat16)
+        return rows.reshape(expert_count, capacity + 2, columns)
+
     sent_p = jnp.sum(jnp.where(match, prob_of[:, None, :], 0.0), axis=2).astype(jnp.bfloat16)
-    p_row = jnp.pad(sent_p, ((0, 0), (0, 2 * columns - capacity)))
-    rows = jnp.where((padded == capacity)[None, :, None], p_row[:, None, :], rows)
-    received = exchange(rows)
+    p_row = jnp.pad(sent_p, ((0, 0), (0, columns - capacity)))
+    x_first = exchange(rows_of(tokens))
+    dy_sent = jnp.where(
+        (padded == capacity)[None, :, None], p_row[:, None, :], rows_of(cotangent)
+    )
+    x_first, dy_sent = lax.optimization_barrier((x_first, dy_sent))
+    received = exchange(dy_sent)
     rows_all = expert_count * capacity
+    x_rows = x_first[:, :capacity].reshape(rows_all, columns)
+    gate_part = jnp.dot(x_rows, gate_w, preferred_element_type=jnp.float32).astype(jnp.bfloat16)
+    up_part = jnp.dot(x_rows, up_w, preferred_element_type=jnp.float32).astype(jnp.bfloat16)
+    others = (lax.psum(gate_part, "dp"), lax.psum(up_part, "dp"))
     gate_probs = received[:, capacity, :capacity].reshape(rows_all).astype(jnp.float32)
-    got = received[:, :capacity].reshape(rows_all, 2 * columns)
-    x_rows, dy_rows = got[:, :columns], got[:, columns:]
-    parts = (
-        jnp.dot(x_rows, gate_w, preferred_element_type=jnp.float32),
-        jnp.dot(x_rows, up_w, preferred_element_type=jnp.float32),
-        contract_columns(dy_rows, down_w),
-    )
-    gate_sum, up_sum, grad_h = (
-        lax.psum(v.astype(jnp.bfloat16), "dp").astype(jnp.float32) for v in parts
-    )
+    dy_rows = received[:, :capacity].reshape(rows_all, columns)
+    cot_part = contract_columns(dy_rows, down_w).astype(jnp.bfloat16)
+    grad_h, others = sum_by_exchange(cot_part, others)
+    gate_sum, up_sum, grad_h = (v.astype(jnp.float32) for v in (*others, grad_h))
     h_scaled, d_gate, d_up, prob_grad = local_step(gate_sum, up_sum, grad_h, gate_probs)
     dx_rows = contract_columns(d_gate, gate_w) + contract_columns(d_up, up_w)
     dx_rows = dx_rows.astype(jnp.bfloat16).reshape(expert_count, capacity, columns)

time: 262 us -> 291 us (1.11)
  starting transfers between devices: 11.6 us -> 37.9 us
  waiting for transfers between devices: 130 us -> 147 us
  blocking collectives: 65.8 us -> 52 us
    psum x1, waiting for transfers between devices: 109 us -> 42.7 us  [local(): others = (lax.psum(gate_part, 'dp'), lax.psum(up_part, 'dp'))]
    all_to_all x1 -> x3, waiting for transfers between devices: 21.2 us -> 69.5 us  [exchange(): lax.all_to_all(rows, 'expert', split_axis=0, concat_axis=0, tiled=True)]
    all_to_all x0 -> x1, waiting for transfers between devices: none -> 34.6 us  [sum_by_exchange(): lax.all_to_all(copies, 'dp', split_axis=0, concat_axis=0, tiled=True)]
    all_to_all x1 -> x3, starting transfers between devices: 11.5 us -> 33.6 us  [exchange(): lax.all_to_all(rows, 'expert', split_axis=0, concat_axis=0, tiled=True)]
    all_to_all x1, blocking collectives: 65.8 us -> 52 us  [sum_by_exchange(): lax.all_to_all(slices, 'dp', split_axis=0, concat_axis=0, tiled=True)]
    all_to_all x0 -> x1, starting transfers between devices: none -> 4.28 us  [sum_by_exchange(): lax.all_to_all(copies, 'dp', split_axis=0, concat_axis=0, tiled=True)]
  transfers between devices with their start and end apart: 2 -> 5, of which waited for: 2 -> 5; matrix products, arithmetic and copies ran while one was open for 3% -> 6% of each run, Pallas kernels for 0% -> 0%
where the time goes in v3:
time: 291 us; the launch traced here: 290 us
  waiting for transfers between devices  147 us (51%)
  blocking collectives  52 us (18%)
  starting transfers between devices  37.9 us (13%)
  matrix products  23.6 us (8%)
  between operations  14.3 us (5%)
  other arithmetic  10.8 us (4%)
  local copies, waits for them, and re-layouts  4.75 us (2%)
    all_to_all x3, waiting for transfers between devices, exchange(): lax.all_to_all(rows, 'expert', split_axis=0, concat_axis=0, tiled=True)  69.5 us
    all_to_all x1, blocking collectives, sum_by_exchange(): lax.all_to_all(slices, 'dp', split_axis=0, concat_axis=0, tiled=True)  52 us
    psum x1, waiting for transfers between devices, local(): others = (lax.psum(gate_part, 'dp'), lax.psum(up_part, 'dp'))  42.7 us
    all_to_all x1, waiting for transfers between devices, sum_by_exchange(): lax.all_to_all(copies, 'dp', split_axis=0, concat_axis=0, tiled=True)  34.6 us
    all_to_all x3, starting transfers between devices, exchange(): lax.all_to_all(rows, 'expert', split_axis=0, concat_axis=0, tiled=True)  33.6 us
    dot_general x4, matrix products, contract_rows(): lax.dot_general(a, b, (((0,), (0,)), ((), ())), preferred_element_type=jn...  10.2 us
  transfers between devices with their start and end apart: 5, of which 5 were waited for; matrix products, arithmetic and copies ran while one was open for 6% of the time, Pallas kernels for 0%

profile of v3, /device:TPU:1, one launch (start us, length us, event | category | flops | bytes accessed | tf_op | source)
XLA Modules:
  0.0 290.2 jit_solution(12262111622484554025)
XLA Ops:
  8.5 2.3 convolution_convert_fusion.4
  10.8 14.8 %all-to-all-start = ((bf16[64,16,512]{2,1,0:T(8,128)(2,1)}), bf16[64,16,512]{2,1,0:T(8,128)(2,1)S(1)}, u32[]{:S(2)}, u32[]{:S(2)}) async-start(bf16[64,16,512]{2,1,0:T(8,128)(2,1)} %bitcast.2), calls=%async_computation | async-start | bytes 2097152 | tf_op jit(solution)/shard_map/all_to_all | solution.py:34
  26.5 1.2 broadcast_select_fusion
  27.7 26.5 %all-to-all-done = bf16[64,16,512]{2,1,0:T(8,128)(2,1)S(1)} async-done(((bf16[64,16,512]{2,1,0:T(8,128)(2,1)}), bf16[64,16,512]{2,1,0:T(8,128)(2,1)S(1)}, u32[]{:S(2)}, u32[]{:S(2)}) %all-to-all-start) | async-done | bytes 1048608 | tf_op jit(solution)/shard_map/all_to_all | solution.py:34
  54.1 6.2 %all-to-all-start.1 = ((bf16[64,16,512]{2,1,0:T(8,128)(2,1)}), bf16[64,16,512]{2,1,0:T(8,128)(2,1)S(1)}, u32[]{:S(2)}, u32[]{:S(2)}) async-start(bf16[64,16,512]{2,1,0:T(8,128)(2,1)} %broadcast_select_fusion), calls=%async_computation.1 | async-start | bytes 2097152 | tf_op jit(solution)/shard_map/all_to_all | solution.py:34
  60.4 1.2 reshape.68
  61.6 3.5 %convolution_convert_fusion = bf16[896,768]{1,0:T(8,128)(2,1)} fusion(bf16[896,512]{1,0:T(8,128)(2,1)} %reshape.68, bf16[1,512,768]{2,1,0:T(8,128)(2,1)} %param.12), kind=kOutput, calls=%fused_computation.21 | convolution fusion | flops 705331200 | bytes 3080192 | tf_op jit(solution)/shard_map/dot_general | solution.py:85
  65.1 2.0 convolution_convert_fusion.1
  67.1 21.8 %all-to-all-done.1 = bf16[64,16,512]{2,1,0:T(8,128)(2,1)S(1)} async-done(((bf16[64,16,512]{2,1,0:T(8,128)(2,1)}), bf16[64,16,512]{2,1,0:T(8,128)(2,1)S(1)}, u32[]{:S(2)}, u32[]{:S(2)}) %all-to-all-start.1) | async-done | bytes 1048608 | tf_op jit(solution)/shard_map/all_to_all | solution.py:34
  90.1 52.0 %all_to_all.25 = bf16[8,112,768]{2,1,0:T(8,128)(2,1)S(1)} all-to-all(bf16[8,112,768]{2,1,0:T(8,128)(2,1)S(1)} %bitcast.63), channel_id=1, replica_groups=mesh['dp'=8,'expert'=64] {'dp'}, dimensions={0} | all-to-all | bytes 2752512 | tf_op jit(solution)/shard_map/all_to_all | solution.py:40
  142.3 42.7 %all-reduce.5.cloned.1.call-done = (bf16[896,768]{1,0:T(8,128)(2,1)}, bf16[896,768]{1,0:T(8,128)(2,1)}) async-done(((bf16[896,768]{1,0:T(8,128)(2,1)}, bf16[896,768]{1,0:T(8,128)(2,1)}), (bf16[896,768]{1,0:T(8,128)(2,1)}, bf16[896,768]{1,0:T(8,128)(2,1)})) %all-reduce.5.cloned.1.call-update) | async-done | bytes 2752528 | tf_op jit(solution)/shard_map/psum | solution.py:86
  186.2 4.3 %all-to-all-start.3 = ((bf16[8,112,768]{2,1,0:T(8,128)(2,1)}), bf16[8,112,768]{2,1,0:T(8,128)(2,1)S(1)}, u32[]{:S(2)}, u32[]{:S(2)}) async-start(bf16[8,112,768]{2,1,0:T(8,128)(2,1)} %broadcast_in_dim.105), calls=%async_computation.3 | async-start | bytes 2752512 | tf_op jit(solution)/shard_map/all_to_all | solution.py:44
  190.7 34.6 %all-to-all-done.3 = bf16[8,112,768]{2,1,0:T(8,128)(2,1)S(1)} async-done(((bf16[8,112,768]{2,1,0:T(8,128)(2,1)}), bf16[8,112,768]{2,1,0:T(8,128)(2,1)S(1)}, u32[]{:S(2)}, u32[]{:S(2)}) %all-to-all-start.3) | async-done | bytes 1376288 | tf_op jit(solution)/shard_map/all_to_all | solution.py:44
  225.3 4.5 %fusion.1 = (bf16[896,768]{1,0:T(8,128)(2,1)}, bf16[896,768]{1,0:T(8,128)(2,1)}, bf16[896,768]{1,0:T(8,128)(2,1)S(1)}) fusion(bf16[8,112,768]{2,1,0:T(8,128)(2,1)S(1)} %all-to-all-done.3, f32[896]{0:T(1024)S(1)} %reshape.70, bf16[896,768]{1,0:T(8,128)(2,1)} %get-tuple-element.14, bf16[896,768]{1,0:T(8,128)(2,1)} %get-tuple-element.13), kind=kLoop, calls=%fused_computation.9 | loop fusion | flops 13074432 | bytes 8261120 | tf_op jit(solution)/shard_map/convert_element_type | solution.py:20
  230.6 2.4 fusion.24
  233.0 1.8 add_convert_fusion
  234.8 1.3 reshape.69
  236.2 1.3 pad_maximum_fusion
  237.5 12.5 %all-to-all-start.4 = ((bf16[64,15,512]{2,1,0:T(8,128)(2,1)}), bf16[64,15,512]{2,1,0:T(8,128)(2,1)}, u32[]{:S(2)}, u32[]{:S(2)}) async-start(bf16[64,15,512]{2,1,0:T(8,128)(2,1)} %pad_maximum_fusion), calls=%async_computation.4 | async-start | bytes 2097152 | tf_op jit(solution)/shard_map/all_to_all | solution.py:34
  250.1 3.2 %fusion.15 = bf16[1,512,768]{2,1,0:T(8,128)(2,1)} fusion(bf16[896,512]{1,0:T(8,128)(2,1)} %reshape.68, bf16[896,768]{1,0:T(8,128)(2,1)S(1)} %copy-done.3), kind=kOutput, calls=%fused_computation.31 | convolution fusion | flops 705036288 | bytes 3080192 | tf_op jit(solution)/shard_map/dot_general | solution.py:26
  253.3 1.9 fusion.14
  255.3 2.0 fusion.16
  257.3 21.2 %all-to-all-done.4 = bf16[64,15,512]{2,1,0:T(8,128)(2,1)} async-done(((bf16[64,15,512]{2,1,0:T(8,128)(2,1)}), bf16[64,15,512]{2,1,0:T(8,128)(2,1)}, u32[]{:S(2)}, u32[]{:S(2)}) %all-to-all-start.4) | async-done | bytes 983072 | tf_op jit(solution)/shard_map/all_to_all | solution.py:34
  279.7 3.0 %fusion.19 = bf16[128,512]{1,0:T(8,128)(2,1)} fusion(bf16[64,14,512]{2,1,0:T(8,128)(2,1)} %bitcast.59, s32[64,128]{1,0:T(8,128)S(1)} %copy-done.9), kind=kOutput, calls=%fused_computation.34 | convolution fusion | flops 117620736 | bytes 1081344 | tf_op jit(solution)/shard_map/dot_general | solution.py:26
  (58 shorter events, 7.4 us)
Async XLA Ops:
  7.2 57.9 %copy-start = (bf16[1,512,768]{2,1,0:T(8,128)(2,1)S(1)}, bf16[1,512,768]{2,1,0:T(8,128)(2,1)}, u32[]{:S(2)}) copy-start(bf16[1,512,768]{2,1,0:T(8,128)(2,1)} %param.11) | copy-start | bytes 2359300
  8.1 17.6 %copy-start.8 = (s32[64,128]{1,0:T(8,128)}, s32[64,128]{1,0:T(8,128)S(1)}, u32[]{:S(2)}) copy-start(s32[64,128]{1,0:T(8,128)S(1)} %fusion.20) | copy-start | bytes 98308
  8.4 17.2 %copy-start.12 = (bf16[128,6]{0,1:T(8,128)(2,1)S(1)}, bf16[128,6]{0,1:T(8,128)(2,1)}, u32[]{:S(2)}) copy-start(bf16[128,6]{0,1:T(8,128)(2,1)} %param.10) | copy-start | bytes 4612
  8.4 17.2 %copy-start.11 = (s32[128,6]{0,1:T(8,128)S(1)}, s32[128,6]{0,1:T(8,128)}, u32[]{:S(2)}) copy-start(s32[128,6]{0,1:T(8,128)} %param.9) | copy-start | bytes 9220
  8.4 17.6 %copy-start.10 = (bf16[128,512]{1,0:T(8,128)(2,1)S(1)}, bf16[128,512]{1,0:T(8,128)(2,1)}, u32[]{:S(2)}) copy-start(bf16[128,512]{1,0:T(8,128)(2,1)} %param.8) | copy-start | bytes 393220
  10.8 43.4 %all-to-all-start = ((bf16[64,16,512]{2,1,0:T(8,128)(2,1)}), bf16[64,16,512]{2,1,0:T(8,128)(2,1)S(1)}, u32[]{:S(2)}, u32[]{:S(2)}) async-start(bf16[64,16,512]{2,1,0:T(8,128)(2,1)} %bitcast.2), calls=%async_computation | async-start | bytes 2097152 | tf_op jit(solution)/shard_map/all_to_all | solution.py:34
  54.1 34.7 %all-to-all-start.1 = ((bf16[64,16,512]{2,1,0:T(8,128)(2,1)}), bf16[64,16,512]{2,1,0:T(8,128)(2,1)S(1)}, u32[]{:S(2)}, u32[]{:S(2)}) async-start(bf16[64,16,512]{2,1,0:T(8,128)(2,1)} %broadcast_select_fusion), calls=%async_computation.1 | async-start | bytes 2097152 | tf_op jit(solution)/shard_map/all_to_all | solution.py:34
  60.4 124.7 %all-reduce.5.cloned.1.call-start = ((), (), s32[]{:S(2)}) async-start(), calls=%async_computation.5 | async-start | bytes 5505024 | tf_op jit(solution)/shard_map/psum | solution.py:86
  61.6 3.5 %copy-start.4 = (bf16[896,512]{1,0:T(8,128)(2,1)S(1)}, bf16[896,512]{1,0:T(8,128)(2,1)}, u32[]{:S(2)}) copy-start(bf16[896,512]{1,0:T(8,128)(2,1)} %reshape.68) | copy-start | bytes 2752516
  67.1 22.1 %copy-start.13 = (bf16[1,768,512]{2,1,0:T(8,128)(2,1)S(1)}, bf16[1,768,512]{2,1,0:T(8,128)(2,1)}, u32[]{:S(2)}) copy-start(bf16[1,768,512]{2,1,0:T(8,128)(2,1)} %param.13) | copy-start | bytes 2359300
  89.2 1.0 copy-start.6
  186.2 39.1 %all-to-all-start.3 = ((bf16[8,112,768]{2,1,0:T(8,128)(2,1)}), bf16[8,112,768]{2,1,0:T(8,128)(2,1)S(1)}, u32[]{:S(2)}, u32[]{:S(2)}) async-start(bf16[8,112,768]{2,1,0:T(8,128)(2,1)} %broadcast_in_dim.105), calls=%async_computation.3 | async-start | bytes 2752512 | tf_op jit(solution)/shard_map/all_to_all | solution.py:44
  230.5 2.4 copy-start.2
  230.6 2.4 copy-start.14
  237.5 12.6 %copy-start.3 = (bf16[896,768]{1,0:T(8,128)(2,1)S(1)}, bf16[896,768]{1,0:T(8,128)(2,1)}, u32[]{:S(2)}) copy-start(bf16[896,768]{1,0:T(8,128)(2,1)} %get-tuple-element.17) | copy-start | bytes 4128772
  237.5 41.0 %all-to-all-start.4 = ((bf16[64,15,512]{2,1,0:T(8,128)(2,1)}), bf16[64,15,512]{2,1,0:T(8,128)(2,1)}, u32[]{:S(2)}, u32[]{:S(2)}) async-start(bf16[64,15,512]{2,1,0:T(8,128)(2,1)} %pad_maximum_fusion), calls=%async_computation.4 | async-start | bytes 2097152 | tf_op jit(solution)/shard_map/all_to_all | solution.py:34
  250.1 3.3 %copy-start.1 = (bf16[896,768]{1,0:T(8,128)(2,1)S(1)}, bf16[896,768]{1,0:T(8,128)(2,1)}, u32[]{:S(2)}) copy-start(bf16[896,768]{1,0:T(8,128)(2,1)} %get-tuple-element.18) | copy-start | bytes 4128772
  250.1 3.3 %copy-start.5 = (bf16[896,512]{1,0:T(8,128)(2,1)S(1)}, bf16[896,512]{1,0:T(8,128)(2,1)}, u32[]{:S(2)}) copy-start(bf16[896,512]{1,0:T(8,128)(2,1)} %reshape.68) | copy-start | bytes 2752516
  253.3 1.9 copy-start.7
  255.3 24.2 %copy-start.9 = (s32[64,128]{1,0:T(8,128)S(1)}, s32[64,128]{1,0:T(8,128)}, u32[]{:S(2)}) copy-start(s32[64,128]{1,0:T(8,128)} %copy-done.8) | copy-start | bytes 98308
Sparse Core Ops, SparseCore 0:
  67.2 117.7 all-reduce.4
